TPU v7x, 256 devices: a whole 4x4x8 slice. The times are simulated.
256 devices in a mesh: seq: 16 (over z, core), dp: 16 (over y, x).
Axes of the slice: x: 4, y: 4, z: 8, core: 2. Of those that a mesh axis runs over, the one named last changes fastest.
Arguments:
- queries: bfloat16 [16, 2048, 1280], P('dp', 'seq'), may hold values from -43 to 43
- key_rows: bfloat16 [16, 2048, 1280], P('dp', 'seq'), may hold values from -7 to 7
- value_rows: bfloat16 [16, 2048, 1280], P('dp', 'seq'), may hold values from -6 to 6
- resid_in: bfloat16 [16, 2048, 1280], P('dp', 'seq'), may hold values from -6 to 6
- llm_grad: bfloat16 [16, 3072, 1280], P('dp', 'seq'), may hold values from -6 to 6
- vision_slot: int32 [16, 3072], P('dp', 'seq'), may hold values from -1 to 2047, as said below
- window_mask: int32 [16, 32, 2], P('dp', 'seq'), may hold values from 0 to 1, as said below
- w_up: bfloat16 [1280, 2560], P('dp'), may hold values from -0.15625 to 0.15625
- w_down: bfloat16 [2560, 1280], P('dp'), may hold values from -0.125 to 0.125
- norm_gain: bfloat16 [1280], P('dp'), may hold values from 0.25 to 1.75
Outputs:
- grad_query: bfloat16 [16, 2048, 1280], P('dp', 'seq')
- grad_key: bfloat16 [16, 2048, 1280], P('dp', 'seq')
- grad_value: bfloat16 [16, 2048, 1280], P('dp', 'seq')
- grad_resid: bfloat16 [16, 2048, 1280], P('dp', 'seq')
- grad_up: bfloat16 [1280, 2560], P('seq', 'dp')
- grad_down: bfloat16 [2560, 1280], P('seq', 'dp')
- grad_gain: float32 [1280], replicated
Inputs may be any that keep to these rules, and one draw needn't show every extreme that they name: `vision_slot`: -1 marks a text position; every vision token of a batch stands at exactly one position. Positions come in aligned runs of 16: each run is text or the 16 consecutive vision tokens of one tile, in order. Each language-model shard holds exactly 8 tiles, and at most 32 vision tokens of one owner; in every batch, for every owner, some shard holds exactly 32 of that owner's vision tokens. `window_mask`: each owner's 2 blocks are split into images of one or more consecutive blocks; a block attends to exactly the blocks of its own image, itself included (entry i % 2 of row i is 1).
All inputs are finite; a program needn't handle non-finite values.
Results may differ from a plain program's by a relative error of at most 0.023.
Values may be sent and summed in bfloat16 or wider, within the bound.
A program may use at most 128 MiB of HBM per device.

v0:
```python
import math
import jax
import jax.numpy as jnp
from jax import lax
from jax.sharding import PartitionSpec as P

HEADS = 16
HDIM = 80
BLK = 64
PIECE = 16


def contract(left, right, left_dim, right_dim):
    return lax.dot_general(
        left, right, (((left_dim,), (right_dim,)), ((), ())), preferred_element_type=jnp.float32
    )


def per_device(
    queries,
    key_rows,
    value_rows,
    resid_in,
    llm_grad,
    vision_slot,
    window_mask,
    w_up,
    w_down,
    norm_gain,
):
    seq_count = lax.axis_size("seq")
    data_count = lax.axis_size("dp")
    query = queries[0]
    key_block = key_rows[0]
    value_block = value_rows[0]
    tokens, feat_dim = query.shape
    att_scale = 1.0 / math.sqrt(HDIM)
    up_full, down_full, gain_full = (
        lax.all_gather(w_up, "dp", axis=0, tiled=True),
        lax.all_gather(w_down, "dp", axis=0, tiled=True),
        lax.all_gather(norm_gain, "dp", axis=0, tiled=True),
    )
    slot_ids = vision_slot[0]
    piece_count = tokens // PIECE
    capacity = PIECE * (1 + (piece_count + seq_count - 2) // seq_count)
    owner_of = jnp.where(slot_ids >= 0, slot_ids // tokens, seq_count)
    onehot = (owner_of[:, None] == jnp.arange(seq_count)[None, :]).astype(jnp.int32)
    ranking = jnp.sum((jnp.cumsum(onehot, axis=0) - 1) * onehot, axis=1)
    target = jnp.where(slot_ids >= 0, owner_of * capacity + ranking, seq_count * capacity)
    send_rows = (
        jnp.zeros((seq_count * capacity, feat_dim), jnp.bfloat16)
        .at[target]
        .set(llm_grad[0], mode="drop")
    )
    send_ids = (
        jnp.full((seq_count * capacity,), -1, jnp.int32)
        .at[target]
        .set(jnp.where(slot_ids >= 0, slot_ids % tokens, -1), mode="drop")
    )
    recv_rows = lax.all_to_all(
        send_rows.reshape(seq_count, capacity, feat_dim),
        "seq",
        split_axis=0,
        concat_axis=0,
        tiled=True,
    )
    recv_ids = lax.all_to_all(
        send_ids.reshape(seq_count, capacity), "seq", split_axis=0, concat_axis=0, tiled=True
    )
    flat_ids = recv_ids.reshape(seq_count * capacity)
    landing = jnp.where(flat_ids >= 0, flat_ids, tokens)
    grad_rows = (
        jnp.zeros((tokens, feat_dim), jnp.bfloat16)
        .at[landing]
        .set(recv_rows.reshape(seq_count * capacity, feat_dim), mode="drop")
    )
    allowed = jnp.repeat(jnp.repeat(window_mask[0] > 0, BLK, axis=0), BLK, axis=1)
    q_heads = query.reshape(tokens, HEADS, HDIM)
    k_heads = key_block.reshape(tokens, HEADS, HDIM)
    v_heads = value_block.reshape(tokens, HEADS, HDIM)
    scores = (
        jnp.einsum("qhd,khd->hqk", q_heads, k_heads, preferred_element_type=jnp.float32) * att_scale
    )
    masked = jnp.where(allowed[None], scores, -jnp.inf)
    highest = jnp.max(masked, axis=2, keepdims=True)
    exp_terms = jnp.where(allowed[None], jnp.exp(masked - highest), 0.0)
    attn_probs = exp_terms / jnp.sum(exp_terms, axis=2, keepdims=True)
    probs_low = attn_probs.astype(jnp.bfloat16)
    attn_heads = jnp.einsum(
        "hqk,khd->qhd", probs_low, v_heads, preferred_element_type=jnp.float32
    ).astype(jnp.bfloat16)
    attn_out = attn_heads.reshape(tokens, feat_dim)
    hidden = resid_in[0].astype(jnp.float32) + attn_out.astype(jnp.float32)
    center = jnp.mean(hidden, axis=1, keepdims=True)
    variance = jnp.mean(jnp.square(hidden - center), axis=1, keepdims=True)
    inverse = lax.rsqrt(variance + 1e-06)
    normal_unit = (hidden - center) * inverse
    gain_wide = gain_full.astype(jnp.float32)
    normed = (normal_unit * gain_wide).astype(jnp.bfloat16)
    pre_act = jnp.dot(normed, up_full, preferred_element_type=jnp.float32)
    sig_gate = jax.nn.sigmoid(1.702 * pre_act)
    act_low = (pre_act * sig_gate).astype(jnp.bfloat16)
    down_term = contract(act_low, grad_rows, 0, 0)
    d_act = contract(grad_rows, down_full, 1, 1)
    d_pre = (d_act * (sig_gate + 1.702 * pre_act * sig_gate * (1.0 - sig_gate))).astype(
        jnp.bfloat16
    )
    d_normed = contract(d_pre, up_full, 1, 1)
    gain_term = jnp.sum(d_normed * normal_unit, axis=0)
    d_unit = d_normed * gain_wide
    d_hidden = inverse * (
        d_unit
        - jnp.mean(d_unit, axis=1, keepdims=True)
        - normal_unit * jnp.mean(d_unit * normal_unit, axis=1, keepdims=True)
    )
    grad_resid = (grad_rows.astype(jnp.float32) + d_hidden).astype(jnp.bfloat16)
    up_term = contract(normed, d_pre, 0, 0)
    grad_heads = grad_resid.reshape(tokens, HEADS, HDIM)
    grad_value = jnp.einsum(
        "hqk,qhd->khd", probs_low, grad_heads, preferred_element_type=jnp.float32
    ).astype(jnp.bfloat16)
    d_probs = jnp.einsum("qhd,khd->hqk", grad_heads, v_heads, preferred_element_type=jnp.float32)
    delta = jnp.einsum("qhd,qhd->hq", grad_heads, attn_heads, preferred_element_type=jnp.float32)
    d_scores = (attn_probs * (d_probs - delta[:, :, None]) * att_scale).astype(jnp.bfloat16)
    grad_query = jnp.einsum(
        "hqk,khd->qhd", d_scores, k_heads, preferred_element_type=jnp.float32
    ).astype(jnp.bfloat16)
    grad_key = jnp.einsum(
        "hqk,qhd->khd", d_scores, q_heads, preferred_element_type=jnp.float32
    ).astype(jnp.bfloat16)
    up_part, down_part = (
        lax.psum_scatter(
            up_term.astype(jnp.bfloat16), "seq", scatter_dimension=0, tiled=True
        ).astype(jnp.float32),
        lax.psum_scatter(
            down_term.astype(jnp.bfloat16), "seq", scatter_dimension=0, tiled=True
        ).astype(jnp.float32),
    )
    up_panel, down_panel = (
        lax.psum_scatter(
            up_part.astype(jnp.bfloat16), "dp", scatter_dimension=1, tiled=True
        ).astype(jnp.float32),
        lax.psum_scatter(
            down_part.astype(jnp.bfloat16), "dp", scatter_dimension=1, tiled=True
        ).astype(jnp.float32),
    )
    factor = 1.0 / math.sqrt(data_count * seq_count * tokens)
    gain_total = lax.psum(gain_term, ("seq", "dp"))
    return (
        grad_query.reshape(1, tokens, feat_dim),
        grad_key.reshape(1, tokens, feat_dim),
        grad_value.reshape(1, tokens, feat_dim),
        grad_resid[None],
        (up_panel * factor).astype(jnp.bfloat16),
        (down_panel * factor).astype(jnp.bfloat16),
        gain_total * factor,
    )


def solution(mesh):
    in_specs = (
        P("dp", "seq", None),
        P("dp", "seq", None),
        P("dp", "seq", None),
        P("dp", "seq", None),
        P("dp", "seq", None),
        P("dp", "seq"),
        P("dp", "seq", None),
        P("dp", None),
        P("dp", None),
        P("dp"),
    )
    out_specs = (
        P("dp", "seq", None),
        P("dp", "seq", None),
        P("dp", "seq", None),
        P("dp", "seq", None),
        P("seq", "dp"),
        P("seq", "dp"),
        P(),
    )
    return jax.shard_map(
        per_device, mesh=mesh, in_specs=in_specs, out_specs=out_specs, check_vma=False
    )
```

profile of v0, /device:TPU:2, one launch (start us, length us, event | category | flops | bytes accessed | tf_op | source)
XLA Modules:
  0.0 466.7 jit_solution(10220901300629912734)
XLA Ops:
  11.0 1.2 scatter_custom_fusion
  12.9 8.6 %all-to-all-start = ((s32[16,1,32]{2,1,0:T(1,128)}), s32[16,1,32]{2,1,0:T(1,128)S(1)}, u32[]{:S(2)}, u32[]{:S(2)}) async-start(s32[16,1,32]{2,1,0:T(1,128)} %all_to_all.9), calls=%async_computation | async-start | bytes 16384 | tf_op jit(solution)/shard_map/all_to_all | solution.py:67
  21.5 2.7 scatter_custom_fusion.1
  24.1 4.9 %all-to-all-done = s32[16,1,32]{2,1,0:T(1,128)S(1)} async-done(((s32[16,1,32]{2,1,0:T(1,128)}), s32[16,1,32]{2,1,0:T(1,128)S(1)}, u32[]{:S(2)}, u32[]{:S(2)}) %all-to-all-start) | async-done | bytes 2080 | tf_op jit(solution)/shard_map/all_to_all | solution.py:67
  29.0 3.8 all-to-all-start.1
  34.4 1.5 fusion.35
  35.9 1.6 convolution_convert_fusion.3
  40.4 37.7 %all-reduce.1 = bf16[1280]{0:T(1024)(128)(2,1)S(1)} all-reduce(bf16[1280]{0:T(1024)(128)(2,1)S(1)} %dynamic-update-slice), channel_id=1, replica_groups=mesh['seq'=16,'dp'=16] {'dp'}, use_global_device_ids=true, to_apply=%add.1 | all-reduce | flops 1280 | bytes 5120
  79.7 2.9 scatter_custom_fusion.2
  82.7 3.9 fusion.31
  86.6 64.3 %all-gather.3.cloned.1.call-done = bf16[2560,1280]{1,0:T(8,128)(2,1)} async-done(((bf16[160,1280]{1,0:T(8,128)(2,1)}), bf16[2560,1280]{1,0:T(8,128)(2,1)}) %all-gather.3.cloned.1.call-update) | async-done | bytes 6553616 | tf_op jit(solution)/shard_map/all_gather | solution.py:40
  151.0 5.1 %fusion.1 = bf16[128,2560]{1,0:T(8,128)(2,1)S(1)} fusion(bf16[128,1280]{1,0:T(8,128)(2,1)S(1)} %scatter_custom_fusion.2, bf16[2560,1280]{1,0:T(8,128)(2,1)} %all-gather.3.cloned.1.call-done, f32[128,2560]{1,0:T(8,128)S(1)} %fusion.31), kind=kOutput, calls=%fused_computation.7 | convolution fusion | flops 842137600 | bytes 8847360 | tf_op jit(solution)/shard_map/dot_general | solution.py:14
  156.1 4.7 convolution_convert_fusion.1
  160.8 4.6 convolution_convert_fusion
  165.5 5.2 %multiply_reduce_fusion = (f32[1280]{0:T(1024)S(1)}, f32[128]{0:T(128)S(1)}, f32[128]{0:T(128)S(1)}, f32[128,1280]{1,0:T(8,128)S(1)}) fusion(f32[128,1280]{1,0:T(8,128)S(1)} %get-tuple-element.32, f32[128]{0:T(128)S(1)} %add_rsqrt_fusion, f32[128]{0:T(128)S(1)} %broadcast_multiply_fusion.3, f32[1280]{0:T(1024)S(1)} %convert_element_type.92, ...), kind=kOutput, calls=%fused_computation.26 | convolution fusion | flops 840169984 | bytes 8531968 | tf_op jit(solution)/shard_map/dot_general | solution.py:14
  170.7 57.6 %reduce-scatter.9.cloned.1.call-done = bf16[80,2560]{1,0:T(8,128)(2,1)} async-done(((bf16[1280,2560]{1,0:T(8,128)(2,1)}), bf16[80,2560]{1,0:T(8,128)(2,1)}) %reduce-scatter.9.cloned.1.call-update) | async-done | bytes 409616 | tf_op jit(solution)/shard_map/reduce_scatter | solution.py:132
  228.3 2.1 copy.80
  231.5 1.7 fusion.8
  233.6 63.2 %reduce-scatter.11.cloned.1.call-done = bf16[160,1280]{1,0:T(8,128)(2,1)} async-done(((bf16[2560,1280]{1,0:T(8,128)(2,1)}), bf16[160,1280]{1,0:T(8,128)(2,1)}) %reduce-scatter.11.cloned.1.call-update) | async-done | bytes 409616 | tf_op jit(solution)/shard_map/reduce_scatter | solution.py:135
  296.7 2.1 copy.82
  299.4 0.9 copy.64
  301.7 0.9 copy.66
  302.6 75.3 %psum.7 = f32[1280]{0:T(1024)S(1)} all-reduce(f32[1280]{0:T(1024)S(1)} %get-tuple-element.28), channel_id=1, replica_groups=mesh['seq'=16,'dp'=16] {'seq','dp'}, use_global_device_ids=true, to_apply=%region_17.18 | all-reduce | flops 1280 | bytes 10240 | tf_op jit(solution)/shard_map/psum | solution.py:148
  380.0 78.3 %reduce-scatter.15.cloned.1.call-done = bf16[80,160]{1,0:T(8,128)(2,1)} async-done(((bf16[1280,160]{1,0:T(8,128)(2,1)}), bf16[80,160]{1,0:T(8,128)(2,1)}) %reduce-scatter.15.cloned.1.call-update) | async-done | bytes 25616
  (97 shorter events, 16.9 us)
Async XLA Ops:
  7.2 14.3 %copy-start = (bf16[1,192,1280]{2,1,0:T(8,128)(2,1)S(1)}, bf16[1,192,1280]{2,1,0:T(8,128)(2,1)}, u32[]{:S(2)}) copy-start(bf16[1,192,1280]{2,1,0:T(8,128)(2,1)} %param.14) | copy-start | bytes 1474564
  7.2 75.5 %all-gather.5.cloned.1.call-start = ((), (), s32[]{:S(2)}) async-start(), calls=%async_computation.7 | async-start | bytes 6963200 | tf_op jit(solution)/shard_map/all_gather | solution.py:39
  7.9 143.1 %all-gather.3.cloned.1.call-start = ((), (), s32[]{:S(2)}) async-start(), calls=%async_computation.6 | async-start | bytes 6963200 | tf_op jit(solution)/shard_map/all_gather | solution.py:40
  12.9 16.1 %all-to-all-start = ((s32[16,1,32]{2,1,0:T(1,128)}), s32[16,1,32]{2,1,0:T(1,128)S(1)}, u32[]{:S(2)}, u32[]{:S(2)}) async-start(s32[16,1,32]{2,1,0:T(1,128)} %all_to_all.9), calls=%async_computation | async-start | bytes 16384 | tf_op jit(solution)/shard_map/all_to_all | solution.py:67
  29.0 3.9 copy-start.8
  29.0 4.1 copy-start.9
  29.0 50.7 %all-to-all-start.1 = ((bf16[16,32,1280]{2,1,0:T(8,128)(2,1)}), bf16[16,32,1280]{2,1,0:T(8,128)(2,1)S(1)}, u32[]{:S(2)}, u32[]{:S(2)}) async-start(bf16[16,32,1280]{2,1,0:T(8,128)(2,1)} %bitcast.13), calls=%async_computation.1 | async-start | bytes 2621440 | tf_op jit(solution)/shard_map/all_to_all | solution.py:60
  32.8 1.0 copy-start.10
  32.9 1.2 copy-start.14
  32.9 195.4 %reduce-scatter.9.cloned.1.call-start = ((), (), s32[]{:S(2)}) async-start(), calls=%async_computation.8 | async-start | bytes 6963200 | tf_op jit(solution)/shard_map/reduce_scatter | solution.py:132
  33.2 2.7 copy-start.3
  33.8 2.0 copy-start.11
  34.0 1.8 copy-start.1
  38.2 1.9 copy-start.15
  38.3 39.8 %copy-start.13 = (bf16[1,128,1280]{2,1,0:T(8,128)(2,1)S(1)}, bf16[1,128,1280]{2,1,0:T(8,128)(2,1)}, u32[]{:S(2)}) copy-start(bf16[1,128,1280]{2,1,0:T(8,128)(2,1)} %param.13) | copy-start | bytes 983044
  160.8 136.0 %reduce-scatter.11.cloned.1.call-start = ((), (), s32[]{:S(2)}) async-start(), calls=%async_computation.9 | async-start | bytes 6963200 | tf_op jit(solution)/shard_map/reduce_scatter | solution.py:135
  165.5 213.0 %reduce-scatter.13.cloned.1.call-start = ((), (), s32[]{:S(2)}) async-start(), calls=%async_computation.10 | async-start | bytes 696320
  230.4 228.0 %reduce-scatter.15.cloned.1.call-start = ((), (), s32[]{:S(2)}) async-start(), calls=%async_computation.11 | async-start | bytes 696320
  230.4 1.0 copy-start.7
  230.4 1.1 copy-start.12
  230.8 2.4 copy-start.5
  231.5 1.7 copy-start.4
  233.2 65.6 %copy-start.2 = (bf16[1,128,1280]{1,2,0:T(8,128)(2,1)S(1)}, bf16[1,128,1280]{1,2,0:T(8,128)(2,1)}, u32[]{:S(2)}) copy-start(bf16[1,128,1280]{1,2,0:T(8,128)(2,1)} %copy-done.1) | copy-start | bytes 983044
  298.9 2.3 copy-start.17
  (2 other events, 1.4 us)
Sparse Core Ops, SparseCore 0:
  10.4 70.4 all-gather.4
  83.3 67.5 all-gather.2
  160.9 67.3 reduce-scatter.8
  230.7 65.9 reduce-scatter.10
  300.1 76.7 reduce-scatter.12
  380.2 78.0 reduce-scatter.14
where the time goes:
time: 467 us
  waiting for transfers between devices  270 us (58%)
  blocking collectives  113 us (24%)
  matrix products  29.6 us (6%)
  local copies, waits for them, and re-layouts  21.1 us (5%)
  between operations  15.1 us (3%)
  starting transfers between devices  12.6 us (3%)
  other arithmetic  5.58 us (1%)
    unnamed x8, waiting for transfers between devices  79.8 us
    psum x1, blocking collectives, per_device(): gain_total = lax.psum(gain_term, ('seq', 'dp'))  75.3 us
    all_gather x1, waiting for transfers between devices, per_device(): lax.all_gather(w_down, 'dp', axis=0, tiled=True)  64.3 us
    reduce_scatter x1, waiting for transfers between devices, per_device(): lax.psum_scatter(down_term.astype(jnp.bfloat16), 'seq', scatter_dimension...  63.2 us
    reduce_scatter x1, waiting for transfers between devices, per_device(): lax.psum_scatter(up_term.astype(jnp.bfloat16), 'seq', scatter_dimension=0...  57.6 us
    unnamed x1, blocking collectives  37.7 us
    dot_general x4, matrix products, contract(): lax.dot_general(left, right, (((left_dim,), (right_dim,)), ((), ())), pre...  19.6 us
    unnamed x49, local copies, waits for them, and re-layouts  12.1 us
  transfers between devices with their start and end apart: 8, of which 5 were waited for; matrix products, arithmetic and copies ran while one was open for 9% of the time, Pallas kernels for 0%

commit v1 on v0

--- a/solution.py
+++ b/solution.py
@@ -8,6 +8,13 @@
 HDIM = 80
 BLK = 64
 PIECE = 16
+
+
+def mix_groups_here(a0):
+    line_up = []
+    for _ in range(lax.axis_size("dp")):
+        line_up.append(a0)
+    return jnp.concatenate(lax.all_to_all(jnp.stack(line_up, axis=0), "dp", 0, 0), axis=0)
 
 
 def contract(left, right, left_dim, right_dim):
@@ -37,7 +44,7 @@
     att_scale = 1.0 / math.sqrt(HDIM)
     up_full, down_full, gain_full = (
         lax.all_gather(w_up, "dp", axis=0, tiled=True),
-        lax.all_gather(w_down, "dp", axis=0, tiled=True),
+        mix_groups_here(w_down),
         lax.all_gather(norm_gain, "dp", axis=0, tiled=True),
     )
     slot_ids = vision_slot[0]

time: 467 us -> 527 us (1.13)
  blocking collectives: 113 us -> 230 us
  waiting for transfers between devices: 270 us -> 206 us
    unnamed x1, blocking collectives: 37.7 us -> 118 us
    all_gather x1 -> x0, waiting for transfers between devices: 64.3 us -> none  [per_device(): lax.all_gather(w_down, 'dp', axis=0, tiled=True)]
    all_to_all x0 -> x1, blocking collectives: none -> 36.3 us  [per_device(): lax.all_to_all(send_rows.reshape(seq_count, capacity, feat_dim), 'seq', s...]
    unnamed x8 -> x7, waiting for transfers between devices: 79.8 us -> 79.2 us
    unnamed x49 -> x51, local copies, waits for them, and re-layouts: 12.1 us -> 12.1 us
  transfers between devices with their start and end apart: 8 -> 7, of which waited for: 5 -> 4; matrix products, arithmetic and copies ran while one was open for 9% -> 8% of each run, Pallas kernels for 0% -> 0%
where the time goes in v1:
time: 527 us
  blocking collectives  230 us (44%)
  waiting for transfers between devices  206 us (39%)
  matrix products  29.5 us (6%)
  local copies, waits for them, and re-layouts  23.6 us (4%)
  starting transfers between devices  16.4 us (3%)
  between operations  14.8 us (3%)
  other arithmetic  5.58 us (1%)
    unnamed x1, blocking collectives  118 us
    unnamed x7, waiting for transfers between devices  79.2 us
    psum x1, blocking collectives, per_device(): gain_total = lax.psum(gain_term, ('seq', 'dp'))  75.6 us
    reduce_scatter x1, waiting for transfers between devices, per_device(): lax.psum_scatter(down_term.astype(jnp.bfloat16), 'seq', scatter_dimension...  63.5 us
    reduce_scatter x1, waiting for transfers between devices, per_device(): lax.psum_scatter(up_term.astype(jnp.bfloat16), 'seq', scatter_dimension=0...  58 us
    all_to_all x1, blocking collectives, per_device(): lax.all_to_all(send_rows.reshape(seq_count, capacity, feat_dim), 'seq', s...  36.3 us
    dot_general x4, matrix products, contract(): lax.dot_general(left, right, (((left_dim,), (right_dim,)), ((), ())), pre...  19.6 us
    unnamed x51, local copies, waits for them, and re-layouts  12.1 us
  transfers between devices with their start and end apart: 7, of which 4 were waited for; matrix products, arithmetic and copies ran while one was open for 8% of the time, Pallas kernels for 0%

profile of v1, /device:TPU:2, one launch (start us, length us, event | category | flops | bytes accessed | tf_op | source)
XLA Modules:
  0.0 526.5 jit_solution(5458158378696916960)
XLA Ops:
  10.3 1.2 scatter_custom_fusion
  12.1 8.6 %all-to-all-start = ((s32[16,1,32]{2,1,0:T(1,128)}), s32[16,1,32]{2,1,0:T(1,128)S(1)}, u32[]{:S(2)}, u32[]{:S(2)}) async-start(s32[16,1,32]{2,1,0:T(1,128)} %all_to_all.12), calls=%async_computation | async-start | bytes 16384 | tf_op jit(solution)/shard_map/all_to_all | solution.py:74
  20.7 1.9 scatter_custom_fusion.1
  22.6 5.6 %all-to-all-done = s32[16,1,32]{2,1,0:T(1,128)S(1)} async-done(((s32[16,1,32]{2,1,0:T(1,128)}), s32[16,1,32]{2,1,0:T(1,128)S(1)}, u32[]{:S(2)}, u32[]{:S(2)}) %all-to-all-start) | async-done | bytes 2080 | tf_op jit(solution)/shard_map/all_to_all | solution.py:74
  28.2 36.3 %all_to_all.19 = bf16[16,32,1280]{2,1,0:T(8,128)(2,1)S(1)} all-to-all(bf16[16,32,1280]{2,1,0:T(8,128)(2,1)S(1)} %bitcast.88), channel_id=1, replica_groups=mesh['seq'=16,'dp'=16] {'seq'}, dimensions={0} | all-to-all | bytes 2621440 | tf_op jit(solution)/shard_map/all_to_all | solution.py:67
  64.6 3.3 stack.2
  67.9 7.6 %all-to-all-start.2 = ((bf16[16,160,1280]{2,1,0:T(8,128)(2,1)}), bf16[16,160,1280]{2,1,0:T(8,128)(2,1)}, u32[]{:S(2)}, u32[]{:S(2)}) async-start(bf16[16,160,1280]{2,1,0:T(8,128)(2,1)} %stack.2), calls=%async_computation.2 | async-start | bytes 13107200 | tf_op jit(solution)/shard_map/all_to_all | solution.py:17
  77.0 1.5 fusion.35
  78.5 1.6 convolution_convert_fusion.3
  83.0 118.4 %all-reduce.1 = bf16[1280]{0:T(1024)(128)(2,1)S(1)} all-reduce(bf16[1280]{0:T(1024)(128)(2,1)S(1)} %dynamic-update-slice), channel_id=1, replica_groups=mesh['seq'=16,'dp'=16] {'dp'}, use_global_device_ids=true, to_apply=%add.1 | all-reduce | flops 1280 | bytes 5120
  203.1 2.9 scatter_custom_fusion.2
  206.0 3.9 fusion.31
  210.0 5.1 fusion.1
  215.1 4.7 convolution_convert_fusion.1
  219.8 4.6 convolution_convert_fusion
  224.5 5.2 multiply_reduce_fusion
  229.7 58.0 %reduce-scatter.9.cloned.1.call-done = bf16[80,2560]{1,0:T(8,128)(2,1)} async-done(((bf16[1280,2560]{1,0:T(8,128)(2,1)}), bf16[80,2560]{1,0:T(8,128)(2,1)}) %reduce-scatter.9.cloned.1.call-update) | async-done | bytes 409616 | tf_op jit(solution)/shard_map/reduce_scatter | solution.py:139
  287.7 2.1 copy.80
  291.0 1.7 fusion.8
  293.0 63.5 %reduce-scatter.11.cloned.1.call-done = bf16[160,1280]{1,0:T(8,128)(2,1)} async-done(((bf16[2560,1280]{1,0:T(8,128)(2,1)}), bf16[160,1280]{1,0:T(8,128)(2,1)}) %reduce-scatter.11.cloned.1.call-update) | async-done | bytes 409616 | tf_op jit(solution)/shard_map/reduce_scatter | solution.py:142
  356.5 2.1 copy.82
  361.4 0.9 copy.66
  362.3 75.6 %psum.7 = f32[1280]{0:T(1024)S(1)} all-reduce(f32[1280]{0:T(1024)S(1)} %get-tuple-element.28), channel_id=1, replica_groups=mesh['seq'=16,'dp'=16] {'seq','dp'}, use_global_device_ids=true, to_apply=%region_17.18 | all-reduce | flops 1280 | bytes 10240 | tf_op jit(solution)/shard_map/psum | solution.py:155
  440.1 78.4 %reduce-scatter.15.cloned.1.call-done = bf16[80,160]{1,0:T(8,128)(2,1)} async-done(((bf16[1280,160]{1,0:T(8,128)(2,1)}), bf16[80,160]{1,0:T(8,128)(2,1)}) %reduce-scatter.15.cloned.1.call-update) | async-done | bytes 25616
  (98 shorter events, 17.1 us)
Async XLA Ops:
  7.2 13.6 %copy-start = (bf16[1,192,1280]{2,1,0:T(8,128)(2,1)S(1)}, bf16[1,192,1280]{2,1,0:T(8,128)(2,1)}, u32[]{:S(2)}) copy-start(bf16[1,192,1280]{2,1,0:T(8,128)(2,1)} %param.14) | copy-start | bytes 1474564
  7.2 198.8 %all-gather.2.cloned.1.call-start = ((), (), s32[]{:S(2)}) async-start(), calls=%async_computation.7 | async-start | bytes 6963200 | tf_op jit(solution)/shard_map/all_gather | solution.py:46
  12.1 16.1 %all-to-all-start = ((s32[16,1,32]{2,1,0:T(1,128)}), s32[16,1,32]{2,1,0:T(1,128)S(1)}, u32[]{:S(2)}, u32[]{:S(2)}) async-start(s32[16,1,32]{2,1,0:T(1,128)} %all_to_all.12), calls=%async_computation | async-start | bytes 16384 | tf_op jit(solution)/shard_map/all_to_all | solution.py:74
  28.2 36.3 %copy-start.8 = (bf16[160,1280]{1,0:T(8,128)(2,1)S(1)}, bf16[160,1280]{1,0:T(8,128)(2,1)}, u32[]{:S(2)}) copy-start(bf16[160,1280]{1,0:T(8,128)(2,1)} %param.18) | copy-start | bytes 1228804
  67.9 7.7 %copy-start.9 = (bf16[1,128,1280]{2,1,0:T(8,128)(2,1)S(1)}, bf16[1,128,1280]{2,1,0:T(8,128)(2,1)}, u32[]{:S(2)}) copy-start(bf16[1,128,1280]{2,1,0:T(8,128)(2,1)} %param.11) | copy-start | bytes 983044
  67.9 7.9 %copy-start.10 = (bf16[1,128,1280]{2,1,0:T(8,128)(2,1)S(1)}, bf16[1,128,1280]{2,1,0:T(8,128)(2,1)}, u32[]{:S(2)}) copy-start(bf16[1,128,1280]{2,1,0:T(8,128)(2,1)} %param.12) | copy-start | bytes 983044
  67.9 142.1 %all-to-all-start.2 = ((bf16[16,160,1280]{2,1,0:T(8,128)(2,1)}), bf16[16,160,1280]{2,1,0:T(8,128)(2,1)}, u32[]{:S(2)}, u32[]{:S(2)}) async-start(bf16[16,160,1280]{2,1,0:T(8,128)(2,1)} %stack.2), calls=%async_computation.2 | async-start | bytes 13107200 | tf_op jit(solution)/shard_map/all_to_all | solution.py:17
  75.5 1.0 copy-start.11
  75.5 1.2 copy-start.15
  75.5 212.2 %reduce-scatter.9.cloned.1.call-start = ((), (), s32[]{:S(2)}) async-start(), calls=%async_computation.8 | async-start | bytes 6963200 | tf_op jit(solution)/shard_map/reduce_scatter | solution.py:139
  75.8 2.7 copy-start.3
  76.5 2.0 copy-start.12
  76.7 1.8 copy-start.1
  80.8 1.9 copy-start.16
  80.8 120.6 %copy-start.14 = (bf16[1,128,1280]{2,1,0:T(8,128)(2,1)S(1)}, bf16[1,128,1280]{2,1,0:T(8,128)(2,1)}, u32[]{:S(2)}) copy-start(bf16[1,128,1280]{2,1,0:T(8,128)(2,1)} %param.13) | copy-start | bytes 983044
  219.8 136.7 %reduce-scatter.11.cloned.1.call-start = ((), (), s32[]{:S(2)}) async-start(), calls=%async_computation.9 | async-start | bytes 6963200 | tf_op jit(solution)/shard_map/reduce_scatter | solution.py:142
  224.5 214.1 %reduce-scatter.13.cloned.1.call-start = ((), (), s32[]{:S(2)}) async-start(), calls=%async_computation.10 | async-start | bytes 696320
  289.8 228.7 %reduce-scatter.15.cloned.1.call-start = ((), (), s32[]{:S(2)}) async-start(), calls=%async_computation.11 | async-start | bytes 696320
  289.9 1.0 copy-start.7
  289.9 1.1 copy-start.13
  290.3 2.4 copy-start.5
  291.0 1.7 copy-start.4
  292.7 65.9 %copy-start.2 = (bf16[1,128,1280]{1,2,0:T(8,128)(2,1)S(1)}, bf16[1,128,1280]{1,2,0:T(8,128)(2,1)}, u32[]{:S(2)}) copy-start(bf16[1,128,1280]{1,2,0:T(8,128)(2,1)} %copy-done.1) | copy-start | bytes 983044
  358.6 2.3 copy-start.18
  (2 other events, 1.4 us)
Sparse Core Ops, SparseCore 0:
  10.4 86.2 all-gather.1
  219.9 67.7 reduce-scatter.8
  290.3 66.1 reduce-scatter.10
  359.8 77.1 reduce-scatter.12
  440.3 78.1 reduce-scatter.14
